TPU v7x, 32 devices: a whole 2x2x4 slice. The times are simulated.
32 devices in a mesh: vir: 8 (over y, x, core), occ: 4 (over z).
Axes of the slice: x: 2, y: 2, z: 4, core: 2. Of those that a mesh axis runs over, the one named last changes fastest.
Arguments:
- perturbation: float32 [10240, 1024], P('vir', 'occ'), may hold values from -6 to 6
- eig_virtual: float32 [10240, 10240], P('vir', 'occ'), may hold values from -0.0625 to 0.0625
- eig_occupied: float32 [1024, 1024], P('occ'), may hold values from -0.1875 to 0.1875
- energy_virtual: float32 [10240], P('occ'), may hold values from 0.5 to 4
- energy_occupied: float32 [1024], replicated, may hold values from -4 to -0.5
Outputs:
- response: float32 [10240, 1024], P('vir', 'occ')
All inputs are finite; a program needn't handle non-finite values.
Results may differ from a plain program's by a relative error of at most 0.000078.
Values sent between devices are 32-bit elements; how exact they have to be, the bound alone decides.
No kernel may reach another device: no remote copies, remote signals or barrier semaphores. Data moves between devices by JAX's collectives and lax.ppermute only.
A program may use at most 128 MiB of HBM per device.

v0:
```python
import jax
import jax.numpy as jnp
from jax import lax
from jax.sharding import PartitionSpec as P


def body(perturbation, eig_virtual, eig_occupied, energy_virtual, energy_occupied):
    exact = lax.Precision.HIGHEST
    share = eig_virtual.shape[1] // lax.axis_size("vir")
    own_energy = lax.dynamic_slice_in_dim(energy_virtual, lax.axis_index("vir") * share, share, 0)
    denominator = own_energy[:, None] - energy_occupied[None, :]
    whole_rows = lax.all_gather(perturbation, "occ", axis=1, tiled=True)
    full_vectors = lax.all_gather(eig_occupied, "occ", axis=0, tiled=True)
    coarse = lax.psum_scatter(
        lax.dot_general(
            eig_virtual,
            whole_rows,
            (((0,), (0,)), ((), ())),
            precision=exact,
            preferred_element_type=jnp.float32,
        ),
        "vir",
        scatter_dimension=0,
        tiled=True,
    )
    projected = jnp.dot(coarse, full_vectors, precision=exact, preferred_element_type=jnp.float32)
    scaled = projected / denominator
    back_rows = lax.dot_general(
        scaled,
        full_vectors,
        (((1,), (1,)), ((), ())),
        precision=exact,
        preferred_element_type=jnp.float32,
    )
    gathered = lax.all_gather(back_rows, "vir", axis=0, tiled=True)
    spread = jnp.dot(eig_virtual, gathered, precision=exact, preferred_element_type=jnp.float32)
    return lax.psum_scatter(spread, "occ", scatter_dimension=1, tiled=True)


def solution(mesh):
    in_specs = (P("vir", "occ"), P("vir", "occ"), P("occ", None), P("occ"), P())
    out_specs = P("vir", "occ")
    return jax.shard_map(body, mesh=mesh, in_specs=in_specs, out_specs=out_specs, check_vma=False)
```

profile of v0, /device:TPU:0, one launch (start us, length us, event | category | flops | bytes accessed | tf_op | source)
XLA Modules:
  0.0 541.2 jit_solution(11509484725248971361)
XLA Ops:
  6.5 0.0 all-gather.4.cloned.1.call-start
  6.5 0.7 all-gather.4.cloned.1.call-update
  7.3 0.0 all-gather.6.cloned.1.call-start
  7.3 0.7 all-gather.6.cloned.1.call-update
  8.0 0.0 reduce-scatter.3.cloned.1.call-start
  8.1 101.6 %all-gather.4.cloned.1.call-done = f32[1280,1024]{1,0:T(8,128)} async-done(((f32[1280,256]{1,0:T(8,128)}), f32[1280,1024]{1,0:T(8,128)}) %all-gather.4.cloned.1.call-update) | async-done | bytes 5242896 | tf_op jit(solution)/shard_map/all_gather | solution.py:12
  109.7 47.1 %fusion = f32[2560,1024]{1,0:T(8,128)} fusion(f32[1280,2560]{1,0:T(8,128)} %param.6, f32[1280,1024]{1,0:T(8,128)} %all-gather.4.cloned.1.call-done), kind=kOutput, calls=%fused_computation.2 | convolution fusion | flops 40265318400 | bytes 28835840 | tf_op jit(solution)/shard_map/dot_general | solution.py:15
  156.8 0.0 copy-start.1
  156.8 0.0 reduce-scatter.3.cloned.1.call-update
  156.8 0.2 all-gather.8.cloned.1.call-start
  157.0 0.8 dynamic_slice.3
  157.8 32.6 %all-gather.6.cloned.1.call-done = f32[1024,1024]{1,0:T(8,128)} async-done(((f32[256,1024]{1,0:T(8,128)}), f32[1024,1024]{1,0:T(8,128)}) %all-gather.6.cloned.1.call-update) | async-done | bytes 4194320 | tf_op jit(solution)/shard_map/all_gather | solution.py:13
  190.4 84.0 %reduce-scatter.3.cloned.1.call-done = f32[320,1024]{1,0:T(8,128)} async-done(((f32[2560,1024]{1,0:T(8,128)}), f32[320,1024]{1,0:T(8,128)}) %reduce-scatter.3.cloned.1.call-update) | async-done | bytes 1310736 | tf_op jit(solution)/shard_map/reduce_scatter | solution.py:14
  274.4 0.0 copy-done.1
  274.4 0.0 copy-start
  274.4 7.2 %convolution_divide_fusion = f32[320,1024]{1,0:T(8,128)S(1)} fusion(f32[320,1024]{1,0:T(8,128)} %reduce-scatter.3.cloned.1.call-done, f32[1024,1024]{1,0:T(8,128)} %all-gather.6.cloned.1.call-done, f32[1024]{0:T(1024)S(1)} %copy-done.1, f32[320]{0:T(512)S(1)} %dynamic_slice.3), kind=kOutput, calls=%fused_computation.1 | convolution fusion | flops 4027187200 | bytes 6821120 | tf_op jit(solution)/shard_map/dot_general | solution.py:26
  281.6 0.0 copy-done
  281.6 5.5 %fusion.1 = f32[320,1024]{1,0:T(8,128)} fusion(f32[320,1024]{1,0:T(8,128)S(1)} %convolution_divide_fusion, f32[1024,1024]{1,0:T(8,128)S(1)} %copy-done), kind=kOutput, calls=%fused_computation.3 | convolution fusion | flops 4026531840 | bytes 6815744 | tf_op jit(solution)/shard_map/dot_general | solution.py:28
  287.1 0.0 all-gather.8.cloned.1.call-update
  287.1 0.0 reduce-scatter.5.cloned.1.call-start
  287.2 63.2 %all-gather.8.cloned.1.call-done = f32[2560,1024]{1,0:T(8,128)} async-done(((f32[320,1024]{1,0:T(8,128)}), f32[2560,1024]{1,0:T(8,128)}) %all-gather.8.cloned.1.call-update) | async-done | bytes 10485776 | tf_op jit(solution)/shard_map/all_gather | solution.py:35
  350.4 87.1 %convolution_bitcast_fusion = f32[1280,1024]{0,1:T(8,128)} fusion(f32[2560,1024]{1,0:T(8,128)} %all-gather.8.cloned.1.call-done, f32[1280,2560]{1,0:T(8,128)} %param.6), kind=kOutput, calls=%fused_computation | convolution fusion | flops 40265318400 | bytes 28835840 | tf_op jit(solution)/shard_map/dot_general | solution.py:36
  437.5 0.0 reduce-scatter.5.cloned.1.call-update
  437.5 93.9 %reduce-scatter.5.cloned.1.call-done = f32[1280,256]{0,1:T(8,128)} async-done(((f32[1280,1024]{0,1:T(8,128)}), f32[1280,256]{0,1:T(8,128)}) %reduce-scatter.5.cloned.1.call-update) | async-done | bytes 1310736 | tf_op jit(solution)/shard_map/reduce_scatter | solution.py:37
  531.5 2.8 copy.6
Async XLA Ops:
  6.5 103.2 %all-gather.4.cloned.1.call-start = ((), (), s32[]{:S(2)}) async-start(), calls=%async_computation.2 | async-start | bytes 6553600 | tf_op jit(solution)/shard_map/all_gather | solution.py:12
  7.3 183.1 %all-gather.6.cloned.1.call-start = ((), (), s32[]{:S(2)}) async-start(), calls=%async_computation.4 | async-start | bytes 5242880 | tf_op jit(solution)/shard_map/all_gather | solution.py:13
  8.0 266.4 %reduce-scatter.3.cloned.1.call-start = ((), (), s32[]{:S(2)}) async-start(), calls=%async_computation.3 | async-start | bytes 11796480 | tf_op jit(solution)/shard_map/reduce_scatter | solution.py:14
  156.8 117.6 %copy-start.1 = (f32[1024]{0:T(1024)S(1)}, f32[1024]{0:T(1024)}, u32[]{:S(2)}) copy-start(f32[1024]{0:T(1024)} %param.9) | copy-start | bytes 12292
  156.8 193.6 %all-gather.8.cloned.1.call-start = ((), (), s32[]{:S(2)}) async-start(), calls=%async_computation.5 | async-start | bytes 11796480 | tf_op jit(solution)/shard_map/all_gather | solution.py:35
  274.4 7.2 %copy-start = (f32[1024,1024]{1,0:T(8,128)S(1)}, f32[1024,1024]{1,0:T(8,128)}, u32[]{:S(2)}) copy-start(f32[1024,1024]{1,0:T(8,128)} %all-gather.6.cloned.1.call-done) | copy-start | bytes 12582916
  287.1 244.3 %reduce-scatter.5.cloned.1.call-start = ((), (), s32[]{:S(2)}) async-start(), calls=%async_computation.6 | async-start | bytes 6553600 | tf_op jit(solution)/shard_map/reduce_scatter | solution.py:37
Sparse Core Ops, SparseCore 0:
  8.9 100.7 all-gather.3
  111.3 79.0 all-gather.5
  193.9 80.4 reduce-scatter.2
  287.3 63.1 all-gather.7
  437.7 93.7 reduce-scatter.4
where the time goes:
time: 549 us; the launch traced here: 541 us
  waiting for transfers between devices  377 us (69%)
  matrix products  147 us (27%)
  between operations  13.5 us (2%)
    all_gather x1, waiting for transfers between devices, body(): whole_rows = lax.all_gather(perturbation, 'occ', axis=1, tiled=True)  102 us
    reduce_scatter x1, waiting for transfers between devices, body(): return lax.psum_scatter(spread, 'occ', scatter_dimension=1, tiled=True)  93.9 us
    dot_general x1, matrix products, body(): jnp.dot(eig_virtual, gathered, precision=exact, preferred_element_type=jn...  87.1 us
    reduce_scatter x1, waiting for transfers between devices, body(): lax.psum_scatter(lax.dot_general(eig_virtual, whole_rows, (((0,), (0,)),...  84 us
    all_gather x1, waiting for transfers between devices, body(): gathered = lax.all_gather(back_rows, 'vir', axis=0, tiled=True)  63.2 us
    dot_general x1, matrix products, body(): lax.dot_general(eig_virtual, whole_rows, (((0,), (0,)), ((), ())), precis...  47.1 us
    all_gather x1, waiting for transfers between devices, body(): full_vectors = lax.all_gather(eig_occupied, 'occ', axis=0, tiled=True)  32.6 us
  transfers between devices with their start and end apart: 5, of which 5 were waited for; matrix products, arithmetic and copies ran while one was open for 9% of the time, Pallas kernels for 0%

commit v1 on v0

--- a/solution.py
+++ b/solution.py
@@ -9,7 +9,21 @@
     share = eig_virtual.shape[1] // lax.axis_size("vir")
     own_energy = lax.dynamic_slice_in_dim(energy_virtual, lax.axis_index("vir") * share, share, 0)
     denominator = own_energy[:, None] - energy_occupied[None, :]
-    whole_rows = lax.all_gather(perturbation, "occ", axis=1, tiled=True)
+    ways, here, step = (lax.axis_size("occ"), lax.axis_index("occ"), perturbation.shape[1])
+    lengths = [n * ways if d == 1 else n for d, n in enumerate(perturbation.shape)]
+    full = lax.dynamic_update_slice_in_dim(
+        jnp.zeros(lengths, perturbation.dtype), perturbation, here * step, axis=1
+    )
+    going_up = going_down = perturbation
+    for far in range(1, ways // 2 + 1):
+        going_up = lax.ppermute(going_up, "occ", [(d, (d + 1) % ways) for d in range(ways)])
+        full = lax.dynamic_update_slice_in_dim(full, going_up, (here - far) % ways * step, axis=1)
+        if 2 * far < ways:
+            going_down = lax.ppermute(going_down, "occ", [(d, (d - 1) % ways) for d in range(ways)])
+            full = lax.dynamic_update_slice_in_dim(
+                full, going_down, (here + far) % ways * step, axis=1
+            )
+    whole_rows = full
     full_vectors = lax.all_gather(eig_occupied, "occ", axis=0, tiled=True)
     coarse = lax.psum_scatter(
         lax.dot_general(

time: 549 us -> 584 us (1.064)
  starting transfers between devices: 0.33 us -> 45.1 us
  waiting for transfers between devices: 377 us -> 349 us
  local copies, waits for them, and re-layouts: 3.56 us -> 18.9 us
    ppermute x0 -> x3, waiting for transfers between devices: none -> 110 us  [the longest x2 77 us: body(): lax.ppermute(going_up, 'occ', [(d, (d + 1) % ways) for d in range(ways)])]
    all_gather x1 -> x0, waiting for transfers between devices: 102 us -> none  [body(): whole_rows = lax.all_gather(perturbation, 'occ', axis=1, tiled=True)]
    reduce_scatter x1 -> x0, waiting for transfers between devices: 84 us -> none  [body(): lax.psum_scatter(lax.dot_general(eig_virtual, whole_rows, (((0,), (0,)),...]
    unnamed x5, waiting for transfers between devices: 1.46 us -> 81.2 us
    ppermute x0 -> x3, starting transfers between devices: none -> 45 us  [the longest x2 42.9 us: body(): lax.ppermute(going_up, 'occ', [(d, (d + 1) % ways) for d in range(ways)])]
    all_gather x1, waiting for transfers between devices: 32.6 us -> 0.01 us  [body(): full_vectors = lax.all_gather(eig_occupied, 'occ', axis=0, tiled=True)]
    unnamed x4 -> x9, local copies, waits for them, and re-layouts: 0.01 us -> 11.4 us
  transfers between devices with their start and end apart: 5 -> 7, of which waited for: 5 -> 6; matrix products, arithmetic and copies ran while one was open for 9% -> 11% of each run, Pallas kernels for 0% -> 0%
where the time goes in v1:
time: 584 us; the launch traced here: 574 us
  waiting for transfers between devices  349 us (60%)
  matrix products  146 us (25%)
  starting transfers between devices  45.1 us (8%)
  local copies, waits for them, and re-layouts  18.9 us (3%)
  between operations  15.3 us (3%)
    reduce_scatter x1, waiting for transfers between devices, body(): return lax.psum_scatter(spread, 'occ', scatter_dimension=1, tiled=True)  93.9 us
    dot_general x1, matrix products, body(): jnp.dot(eig_virtual, gathered, precision=exact, preferred_element_type=jn...  87.1 us
    unnamed x5, waiting for transfers between devices  81.2 us
    ppermute x2, waiting for transfers between devices, body(): lax.ppermute(going_up, 'occ', [(d, (d + 1) % ways) for d in range(ways)])  77 us
    all_gather x1, waiting for transfers between devices, body(): gathered = lax.all_gather(back_rows, 'vir', axis=0, tiled=True)  63.1 us
    dot_general x1, matrix products, body(): lax.dot_general(eig_virtual, whole_rows, (((0,), (0,)), ((), ())), precis...  46.5 us
    ppermute x2, starting transfers between devices, body(): lax.ppermute(going_up, 'occ', [(d, (d + 1) % ways) for d in range(ways)])  42.9 us
    ppermute x1, waiting for transfers between devices, body(): lax.ppermute(going_down, 'occ', [(d, (d - 1) % ways) for d in range(ways)])  33.4 us
  transfers between devices with their start and end apart: 7, of which 6 were waited for; matrix products, arithmetic and copies ran while one was open for 11% of the time, Pallas kernels for 0%

profile of v1, /device:TPU:0, one launch (start us, length us, event | category | flops | bytes accessed | tf_op | source)
XLA Modules:
  0.0 574.3 jit_solution(6018823540006822388)
XLA Ops:
  7.4 0.0 all-gather.3.cloned.1.call-start
  7.4 0.7 all-gather.3.cloned.1.call-update
  8.1 0.0 reduce-scatter.7.cloned.1.call-start
  8.1 3.1 collective-permute-start
  11.2 2.1 collective-permute-start.1
  13.3 47.6 %collective-permute-done = f32[1280,256]{1,0:T(8,128)S(1)} collective-permute-done((f32[1280,256]{1,0:T(8,128)}, f32[1280,256]{1,0:T(8,128)S(1)}, u32[]{:S(2)}, u32[]{:S(2)}) %collective-permute-start) | collective-permute-done | bytes 1310752 | tf_op jit(solution)/shard_map/ppermute | solution.py:19
  61.0 39.8 %collective-permute-start.2 = (f32[1280,256]{1,0:T(8,128)S(1)}, f32[1280,256]{1,0:T(8,128)}, u32[]{:S(2)}, u32[]{:S(2)}) collective-permute-start(f32[1280,256]{1,0:T(8,128)S(1)} %collective-permute-done), channel_id=1, source_target_pairs={{0,1},{1,2},{2,3},{3,0},{4,5},{5,6},{6,7},{7,4},{8,9},{9,10},{10,1... | collective-permute-start | bytes 3932168 | tf_op jit(solution)/shard_map/ppermute | solution.py:19
  100.8 0.6 broadcast_in_dim.2
  101.4 0.0 copy-done.1
  101.4 0.2 constant_dynamic-update-slice_fusion.3
  101.6 0.2 constant_dynamic-update-slice_fusion.2
  101.8 33.4 %collective-permute-done.1 = f32[1280,256]{1,0:T(8,128)} collective-permute-done((f32[1280,256]{1,0:T(8,128)}, f32[1280,256]{1,0:T(8,128)}, u32[]{:S(2)}, u32[]{:S(2)}) %collective-permute-start.1) | collective-permute-done | bytes 1310752 | tf_op jit(solution)/shard_map/ppermute | solution.py:22
  135.2 1.5 constant_dynamic-update-slice_fusion.1
  136.7 29.3 %collective-permute-done.2 = f32[1280,256]{1,0:T(8,128)} collective-permute-done((f32[1280,256]{1,0:T(8,128)S(1)}, f32[1280,256]{1,0:T(8,128)}, u32[]{:S(2)}, u32[]{:S(2)}) %collective-permute-start.2) | collective-permute-done | bytes 1310752 | tf_op jit(solution)/shard_map/ppermute | solution.py:19
  166.0 1.5 constant_dynamic-update-slice_fusion
  167.5 0.0 copy-done.2
  167.5 46.5 %convolution_bitcast_fusion = f32[2560,1024]{0,1:T(8,128)} fusion(f32[1280,1024]{1,0:T(8,128)S(1)} %constant_dynamic-update-slice_fusion, f32[1280,2560]{1,0:T(8,128)S(1)} %copy-done.2), kind=kOutput, calls=%fused_computation | convolution fusion | flops 40265318400 | bytes 28835840 | tf_op jit(solution)/shard_map/dot_general | solution.py:29
  213.9 11.4 %copy.8 = f32[2560,1024]{1,0:T(8,128)} copy(f32[2560,1024]{0,1:T(8,128)} %convolution_bitcast_fusion) | data formatting | bytes 20971520
  225.3 0.0 reduce-scatter.7.cloned.1.call-update
  225.4 0.0 all-gather.5.cloned.1.call-start
  225.4 0.8 dynamic_slice.3
  226.2 80.4 %reduce-scatter.7.cloned.1.call-done = f32[320,1024]{1,0:T(8,128)} async-done(((f32[2560,1024]{1,0:T(8,128)}), f32[320,1024]{1,0:T(8,128)}) %reduce-scatter.7.cloned.1.call-update) | async-done | bytes 1310736
  306.6 7.3 %convolution_divide_fusion = f32[320,1024]{1,0:T(8,128)S(1)} fusion(f32[320,1024]{1,0:T(8,128)} %reduce-scatter.7.cloned.1.call-done, f32[1024,1024]{1,0:T(8,128)} %all-gather.3.cloned.1.call-done, f32[1024]{0:T(1024)S(1)} %copy-done.3, f32[320]{0:T(512)S(1)} %dynamic_slice.3), kind=kOutput, calls=%fused_computation.2 | convolution fusion | flops 4027187200 | bytes 6821120 | tf_op jit(solution)/shard_map/dot_general | solution.py:40
  314.0 0.0 copy-done
  314.0 5.5 fusion
  319.5 0.0 all-gather.5.cloned.1.call-update
  319.6 0.0 reduce-scatter.5.cloned.1.call-start
  319.6 63.1 %all-gather.5.cloned.1.call-done = f32[2560,1024]{1,0:T(8,128)} async-done(((f32[320,1024]{1,0:T(8,128)}), f32[2560,1024]{1,0:T(8,128)}) %all-gather.5.cloned.1.call-update) | async-done | bytes 10485776 | tf_op jit(solution)/shard_map/all_gather | solution.py:49
  382.7 87.1 %convolution_bitcast_fusion.1 = f32[1280,1024]{0,1:T(8,128)} fusion(f32[2560,1024]{1,0:T(8,128)} %all-gather.5.cloned.1.call-done, f32[1280,2560]{1,0:T(8,128)} %param.6), kind=kOutput, calls=%fused_computation.1 | convolution fusion | flops 40265318400 | bytes 28835840 | tf_op jit(solution)/shard_map/dot_general | solution.py:50
  469.8 0.0 reduce-scatter.5.cloned.1.call-update
  469.8 93.9 %reduce-scatter.5.cloned.1.call-done = f32[1280,256]{0,1:T(8,128)} async-done(((f32[1280,1024]{0,1:T(8,128)}), f32[1280,256]{0,1:T(8,128)}) %reduce-scatter.5.cloned.1.call-update) | async-done | bytes 1310736 | tf_op jit(solution)/shard_map/reduce_scatter | solution.py:51
  563.7 2.8 copy.7
  (6 shorter events, 0.0 us)
Async XLA Ops:
  7.4 94.0 %copy-start.1 = (f32[1280,256]{1,0:T(8,128)S(1)}, f32[1280,256]{1,0:T(8,128)}, u32[]{:S(2)}) copy-start(f32[1280,256]{1,0:T(8,128)} %param.5) | copy-start | bytes 3932164
  7.4 218.8 %all-gather.3.cloned.1.call-start = ((), (), s32[]{:S(2)}) async-start(), calls=%async_computation.2 | async-start | bytes 5242880 | tf_op jit(solution)/shard_map/all_gather | solution.py:27
  8.1 298.5 %reduce-scatter.7.cloned.1.call-start = ((), (), s32[]{:S(2)}) async-start(), calls=%async_computation.5 | async-start | bytes 11796480
  8.1 52.8 %collective-permute-start = (f32[1280,256]{1,0:T(8,128)}, f32[1280,256]{1,0:T(8,128)S(1)}, u32[]{:S(2)}, u32[]{:S(2)}) collective-permute-start(f32[1280,256]{1,0:T(8,128)} %param.5), channel_id=1, source_target_pairs={{0,1},{1,2},{2,3},{3,0},{4,5},{5,6},{6,7},{7,4},{8,9},{9,10},{10,1... | collective-permute-start | bytes 3932168 | tf_op jit(solution)/shard_map/ppermute | solution.py:19
  11.2 123.9 %collective-permute-start.1 = (f32[1280,256]{1,0:T(8,128)}, f32[1280,256]{1,0:T(8,128)}, u32[]{:S(2)}, u32[]{:S(2)}) collective-permute-start(f32[1280,256]{1,0:T(8,128)} %param.5), channel_id=1, source_target_pairs={{0,3},{1,0},{2,1},{3,2},{4,7},{5,4},{6,5},{7,6},{8,11},{9,8},{10,9... | collective-permute-start | bytes 3932168 | tf_op jit(solution)/shard_map/ppermute | solution.py:22
  61.0 105.0 %collective-permute-start.2 = (f32[1280,256]{1,0:T(8,128)S(1)}, f32[1280,256]{1,0:T(8,128)}, u32[]{:S(2)}, u32[]{:S(2)}) collective-permute-start(f32[1280,256]{1,0:T(8,128)S(1)} %collective-permute-done), channel_id=1, source_target_pairs={{0,1},{1,2},{2,3},{3,0},{4,5},{5,6},{6,7},{7,4},{8,9},{9,10},{10,1... | collective-permute-start | bytes 3932168 | tf_op jit(solution)/shard_map/ppermute | solution.py:19
  100.7 66.7 %copy-start.2 = (f32[1280,2560]{1,0:T(8,128)S(1)}, f32[1280,2560]{1,0:T(8,128)}, u32[]{:S(2)}) copy-start(f32[1280,2560]{1,0:T(8,128)} %param.6) | copy-start | bytes 39321604
  225.3 81.3 %copy-start.3 = (f32[1024]{0:T(1024)S(1)}, f32[1024]{0:T(1024)}, u32[]{:S(2)}) copy-start(f32[1024]{0:T(1024)} %param.9) | copy-start | bytes 12292
  225.4 157.3 %all-gather.5.cloned.1.call-start = ((), (), s32[]{:S(2)}) async-start(), calls=%async_computation.3 | async-start | bytes 11796480 | tf_op jit(solution)/shard_map/all_gather | solution.py:49
  306.6 7.4 %copy-start = (f32[1024,1024]{1,0:T(8,128)S(1)}, f32[1024,1024]{1,0:T(8,128)}, u32[]{:S(2)}) copy-start(f32[1024,1024]{1,0:T(8,128)} %all-gather.3.cloned.1.call-done) | copy-start | bytes 12582916
  319.6 244.2 %reduce-scatter.5.cloned.1.call-start = ((), (), s32[]{:S(2)}) async-start(), calls=%async_computation.4 | async-start | bytes 6553600 | tf_op jit(solution)/shard_map/reduce_scatter | solution.py:51
Sparse Core Ops, SparseCore 0:
  9.7 150.6 all-gather.2
  469.9 93.7 reduce-scatter.4
Sparse Core Ops, SparseCore 1:
  225.4 81.1 reduce-scatter.6
  319.6 63.0 all-gather.4
